TPU v7x, 32 devices: a whole 2x2x4 slice. The times are simulated.
32 devices in a mesh: dp: 2 (over y), fsdp: 16 (over z, x, core).
Axes of the slice: x: 2, y: 2, z: 4, core: 2. Of those that a mesh axis runs over, the one named last changes fastest.
Arguments:
- ids: int32 [2, 192], P('dp'), may hold values from 0 to 511
- embed: bfloat16 [512, 8192], P(None, 'fsdp'), may hold values from -32 to 32
- gain: bfloat16 [8192], P('fsdp'), may hold values from 0.099609375 to 1.8984375
- w_in: bfloat16 [3, 4096, 8192], P(None, 'fsdp'), may hold values from -0.0625 to 0.0625
- feat_filter: float32 [3, 256, 7], P(None, 'fsdp'), may hold values from -2.4 to 2.4
- inner_filter: float32 [256, 7], P('fsdp'), may hold values from -2.4 to 2.4
- w_out: bfloat16 [4096, 8192], P(None, 'fsdp'), may hold values from -0.09375 to 0.09375
- cotangent: bfloat16 [2, 192, 8192], P('dp', None, 'fsdp'), may hold values from -6 to 6
- right_prev: bfloat16 [8192, 256], P('fsdp'), may hold values from -6 to 6
Outputs:
- block_out: bfloat16 [2, 192, 8192], P('dp', None, 'fsdp')
- filter_grad: float32 [4, 256, 7], P(None, 'fsdp')
- basis: bfloat16 [4096, 256], P('fsdp')
- right_factor: float32 [8192, 256], P('fsdp')
All inputs are finite; a program needn't handle non-finite values.
Results may differ from a plain program's by a relative error of at most 0.014.
The roundings to bfloat16 on the way count: a program that leaves them out, or rounds other values in their place, can miss the bound.
Values may be sent and summed in bfloat16 or wider, within the bound.
No kernel may reach another device: no remote copies, remote signals or barrier semaphores. Data moves between devices by JAX's collectives and lax.ppermute only.
A program may use at most 128 MiB of HBM per device.

v0:
```python
import jax
import jax.numpy as jnp
from jax import lax
from jax.sharding import PartitionSpec as P

D = 8192
C = 4096
GROUP = 16


def shifted(signal, lag, tap_count):
    padded = jnp.pad(signal, ((tap_count - 1, 0), (0, 0)))
    first = tap_count - 1 - lag
    return padded[first : first + signal.shape[0]]


def causal(signal, tap_table):
    tap_count = tap_table.shape[0]
    result = jnp.zeros(signal.shape, jnp.float32)
    for lag in range(tap_count):
        result = result + tap_table[lag][None, :] * shifted(signal, lag, tap_count)
    return result


def anticausal(signal, tap_table):
    tap_count = tap_table.shape[0]
    padded = jnp.pad(signal, ((0, tap_count - 1), (0, 0)))
    result = jnp.zeros(signal.shape, jnp.float32)
    for lag in range(tap_count):
        result = result + tap_table[lag][None, :] * padded[lag : lag + signal.shape[0]]
    return result


def tap_sums(gradient, signal, tap_count):
    listing = []
    for lag in range(tap_count):
        listing.append(jnp.sum(gradient * shifted(signal, lag, tap_count), axis=0))
    stacked = jnp.stack(listing, axis=0)
    grouped = stacked.reshape(tap_count, stacked.shape[1] // GROUP, GROUP).sum(axis=2)
    return grouped.T


def expand(filters):
    return jnp.repeat(filters.T, GROUP, axis=1)


def per_device(ids, embed, gain, w_in, feat_filter, inner_filter, w_out, cotangent, right_prev):
    tokens = ids[0]
    length = tokens.shape[0]
    tap_count = inner_filter.shape[1]
    onehot = (tokens[:, None] == jnp.arange(embed.shape[0], dtype=jnp.int32)[None, :]).astype(
        jnp.bfloat16
    )
    x_cols = jnp.dot(onehot, embed, preferred_element_type=jnp.float32)
    square_sums = lax.psum(jnp.sum(x_cols * x_cols, axis=1), "fsdp")
    factor = lax.rsqrt(square_sums / D + 1e-05)
    normed_cols = (x_cols * factor[:, None] * gain.astype(jnp.float32)[None, :]).astype(
        jnp.bfloat16
    )
    projected = jnp.einsum(
        "ld,kcd->klc",
        lax.all_gather(normed_cols, "fsdp", axis=1, tiled=True),
        w_in,
        preferred_element_type=jnp.float32,
    )
    rounded = lax.optimization_barrier(projected.astype(jnp.bfloat16)).astype(jnp.float32)
    query, key_in, value = (rounded[0], rounded[1], rounded[2])
    query_conv = causal(query, expand(feat_filter[0]))
    key_conv = causal(key_in, expand(feat_filter[1]))
    value_conv = causal(value, expand(feat_filter[2]))
    gated = key_conv * value_conv
    inner_table = expand(inner_filter)
    window = causal(gated, inner_table)
    gated_out = (query_conv * window).astype(jnp.bfloat16)
    cot_cols = cotangent[0]
    shard_piece = lax.all_gather(gated_out, "fsdp", axis=1, tiled=True)
    weight_rows = w_out
    mixed_sum = jnp.dot(shard_piece, weight_rows, preferred_element_type=jnp.float32)
    term = jnp.einsum("lc,ld->cd", shard_piece, cot_cols, preferred_element_type=jnp.float32)
    mixed_sum, grad_part = (mixed_sum, term)
    block_out = (x_cols + mixed_sum).astype(jnp.bfloat16)[None]
    weight_rows = w_out
    mixed_grad = lax.psum_scatter(
        jnp.einsum("cd,ld->cl", weight_rows, cot_cols, preferred_element_type=jnp.float32),
        "fsdp",
        scatter_dimension=0,
        tiled=True,
    ).T
    query_grad = mixed_grad * window
    window_grad = mixed_grad * query_conv
    gated_grad = anticausal(window_grad, inner_table)
    key_grad = gated_grad * value_conv
    value_grad = gated_grad * key_conv
    norm_factor = 1.0 / jnp.sqrt(jnp.float32(lax.axis_size("dp") * length))
    filter_part = (
        jnp.stack(
            [
                tap_sums(query_grad, query, tap_count),
                tap_sums(key_grad, key_in, tap_count),
                tap_sums(value_grad, value, tap_count),
                tap_sums(window_grad, gated, tap_count),
            ],
            axis=0,
        )
        * norm_factor
    )
    grad_total, filter_grad = (
        lax.psum(grad_part.astype(jnp.bfloat16), "dp").astype(jnp.float32),
        lax.psum(filter_part.astype(jnp.bfloat16), "dp").astype(jnp.float32),
    )
    grad_half = grad_total.astype(jnp.bfloat16)
    grad_rows_own = lax.all_to_all(grad_half, "fsdp", split_axis=0, concat_axis=1, tiled=True)
    panel_own = jnp.dot(
        grad_rows_own,
        lax.all_gather(right_prev, "fsdp", axis=0, tiled=True),
        preferred_element_type=jnp.float32,
    ).astype(jnp.bfloat16)
    root_scale = jnp.sqrt(jnp.float32(C))
    gram_local = jnp.einsum("cr,cs->rs", panel_own, panel_own, preferred_element_type=jnp.float32)
    gram_matrix = lax.psum(gram_local, "fsdp")
    lower_factor = jnp.linalg.cholesky(gram_matrix)
    solved = jax.scipy.linalg.solve_triangular(
        lower_factor, panel_own.astype(jnp.float32).T, lower=True
    ).T
    basis_own = (solved * root_scale).astype(jnp.bfloat16)
    right_raw = jnp.einsum(
        "cd,cr->dr",
        grad_half,
        lax.all_gather(basis_own, "fsdp", axis=0, tiled=True),
        preferred_element_type=jnp.float32,
    )
    column_sums = lax.psum(jnp.sum(right_raw * right_raw, axis=0), "fsdp")
    right_factor = right_raw * lax.rsqrt(column_sums / D + 1e-06)[None, :]
    return (block_out, filter_grad, basis_own, right_factor)


def solution(mesh):
    placed = (
        P("dp", None),
        P(None, "fsdp"),
        P("fsdp"),
        P(None, "fsdp", None),
        P(None, "fsdp", None),
        P("fsdp", None),
        P(None, "fsdp"),
        P("dp", None, "fsdp"),
        P("fsdp", None),
    )
    return jax.shard_map(
        per_device,
        mesh=mesh,
        in_specs=placed,
        out_specs=(P("dp", None, "fsdp"), P(None, "fsdp", None), P("fsdp", None), P("fsdp", None)),
        check_vma=False,
    )
```

profile of v0, /device:TPU:0, one launch (start us, length us, event | category | flops | bytes accessed | tf_op | source)
XLA Modules:
  0.0 699.4 jit_solution(17935779332028869934)
XLA Ops:
  7.2 0.7 convert_element_type.108
  8.0 0.3 copy-done
  8.2 1.1 multiply_reduce_fusion.1
  9.3 34.9 %psum.35 = f32[192]{0:T(256)S(1)} all-reduce(f32[192]{0:T(256)S(1)} %get-tuple-element.121), channel_id=1, replica_groups=mesh['dp'=2,'fsdp'=16] {'fsdp'}, use_global_device_ids=true, to_apply=%region_1.0 | all-reduce | flops 192 | bytes 1536 | tf_op jit(solution)/shard_map/psum | solution.py:55
  44.2 0.8 multiply_convert_fusion
  45.1 5.4 fusion.14
  55.0 34.7 %all-gather.5.cloned.1.call-done = bf16[192,8192]{1,0:T(8,128)(2,1)} async-done(((bf16[192,512]{1,0:T(8,128)(2,1)}), bf16[192,8192]{1,0:T(8,128)(2,1)}) %all-gather.5.cloned.1.call-update) | async-done | bytes 3145744 | tf_op jit(solution)/shard_map/all_gather | solution.py:62
  89.7 9.8 %fusion.6 = bf16[3,192,256]{2,1,0:T(8,128)(2,1)S(1)} fusion(bf16[3,256,8192]{2,1,0:T(8,128)(2,1)} %param.12, bf16[192,8192]{1,0:T(8,128)(2,1)} %all-gather.5.cloned.1.call-done), kind=kOutput, calls=%fused_computation.8 | convolution fusion | flops 2416066560 | bytes 16023552 | tf_op jit(solution)/shard_map/ld,kcd->klc/dot_general | solution.py:60
  99.6 58.3 %reduce-scatter.2.cloned.1.call-done = f32[256,192]{0,1:T(8,128)} async-done(((f32[4096,192]{0,1:T(8,128)}), f32[256,192]{0,1:T(8,128)}) %reduce-scatter.2.cloned.1.call-update) | async-done | bytes 196624 | tf_op jit(solution)/shard_map/reduce_scatter | solution.py:83
  158.0 1.1 bitcast_multiply_fusion
  159.1 1.0 fusion.28
  160.1 0.8 fusion.29
  161.0 2.6 multiply_reduce_fusion.23
  163.5 0.7 multiply_convert_fusion.1
  164.3 38.0 %all-gather.7.cloned.1.call-done = bf16[192,4096]{1,0:T(8,128)(2,1)} async-done(((bf16[192,256]{1,0:T(8,128)(2,1)}), bf16[192,4096]{1,0:T(8,128)(2,1)}) %all-gather.7.cloned.1.call-update) | async-done | bytes 1572880 | tf_op jit(solution)/shard_map/all_gather | solution.py:76
  202.3 4.7 convolution_convert_fusion
  207.1 0.5 all-gather.9.cloned.1.call-update
  207.7 106.5 %all-reduce.9.cloned.1.call-done = bf16[4096,512]{1,0:T(8,128)(2,1)} async-done(((bf16[4096,512]{1,0:T(8,128)(2,1)}), bf16[4096,512]{1,0:T(8,128)(2,1)}) %all-reduce.9.cloned.1.call-update) | async-done | bytes 4194320 | tf_op jit(solution)/shard_map/psum | solution.py:108
  314.2 6.4 copy.22
  320.6 5.7 all-to-all-start
  326.3 94.7 %all-gather.9.cloned.1.call-done = bf16[8192,256]{1,0:T(8,128)(2,1)} async-done(((bf16[512,256]{1,0:T(8,128)(2,1)}), bf16[8192,256]{1,0:T(8,128)(2,1)}) %all-gather.9.cloned.1.call-update) | async-done | bytes 4194320 | tf_op jit(solution)/shard_map/all_gather | solution.py:115
  421.0 6.5 all-to-all-done
  427.4 4.8 convolution_convert_fusion.1
  432.2 0.9 fusion.31
  433.2 0.2 all-gather.11.cloned.1.call-start
  433.4 0.6 iota_multiply_fusion
  434.0 103.0 %all-reduce.11.cloned.1.call-done = f32[256,256]{0,1:T(8,128)} async-done(((f32[256,256]{0,1:T(8,128)}), f32[256,256]{0,1:T(8,128)}) %all-reduce.11.cloned.1.call-update) | async-done | bytes 262160 | tf_op jit(solution)/shard_map/psum | solution.py:120
  537.0 1.8 copy.24
  538.8 1.1 fusion.12
  539.9 0.7 copy-done.6
  540.6 11.7 %cholesky.50 = f32[128,128]{1,0:T(8,128)S(1)} custom-call(f32[128,128]{1,0:T(8,128)S(1)} %cholesky.118), custom_call_target="Cholesky" | custom-call | tf_op jit(solution)/shard_map/jit(cholesky)/cholesky | solution.py:121
  552.3 0.6 select_reduce_fusion.1
  552.9 0.7 cholesky.113
  553.6 9.8 %custom-call.15 = f32[1,128,128]{1,2,0:T(8,128)S(1)} custom-call(f32[1,128,128]{2,1,0:T(8,128)S(1)} %get-tuple-element.89), custom_call_target="InvertDiagBlocksLowerTriangular" | custom-call | tf_op jit(solution)/shard_map/jit(cholesky)/cholesky | solution.py:121
  563.4 1.7 constant_dynamic-update-slice_fusion.29
  565.1 1.1 convolution_subtract_fusion.1
  566.2 11.7 %cholesky.105 = f32[128,128]{1,0:T(8,128)S(1)} custom-call(f32[128,128]{1,0:T(8,128)S(1)} %convolution_subtract_fusion.1), custom_call_target="Cholesky" | custom-call | tf_op jit(solution)/shard_map/jit(cholesky)/cholesky | solution.py:121
  577.9 1.3 compare_reduce_fusion.1
  579.2 0.6 select_reduce_fusion
  579.8 0.7 compare_reduce_fusion
  581.7 1.7 select_select_fusion
  583.4 0.7 triangular_solve.59
  584.2 6.8 while.1
  584.2 0.6 fusion.49
  584.8 2.9 bitcast_dynamic-update-slice_fusion.2
  587.6 0.6 fusion.49
  588.2 2.8 bitcast_dynamic-update-slice_fusion.2
  591.0 20.5 %custom-call.16 = f32[2,128,128]{1,2,0:T(8,128)S(1)} custom-call(f32[2,128,128]{2,1,0:T(8,128)} %get-tuple-element.11), custom_call_target="InvertDiagBlocksLowerTriangular" | custom-call | tf_op jit(solution)/shard_map/jit(_solve_triangular)/triangular_solve | solution.py:122
  611.5 0.3 fusion.22
  611.8 1.2 convolution_subtract_fusion
  613.0 0.3 fusion.21
  613.3 0.7 fusion.19
  614.0 1.9 multiply_reduce_fusion.2
  616.6 2.0 multiply_reduce_fusion.29
  620.1 0.8 stack.112
  620.9 0.8 stack.113
  622.1 5.0 psum.36
  627.2 0.6 copy.26
  627.8 3.8 fusion.9
  631.6 0.8 copy.27
  632.4 23.5 %all-gather.11.cloned.1.call-done = bf16[4096,256]{0,1:T(8,128)(2,1)} async-done(((bf16[256,256]{0,1:T(8,128)(2,1)}), bf16[4096,256]{0,1:T(8,128)(2,1)}) %all-gather.11.cloned.1.call-update) | async-done | bytes 2097168 | tf_op jit(solution)/shard_map/all_gather | solution.py:129
  655.9 4.2 multiply_reduce_fusion
  660.1 31.6 %psum.39 = f32[256]{0:T(256)S(1)} all-reduce(f32[256]{0:T(256)S(1)} %get-tuple-element.125), channel_id=1, replica_groups=mesh['dp'=2,'fsdp'=16] {'fsdp'}, use_global_device_ids=true, to_apply=%region_43.44 | all-reduce | flops 256 | bytes 2048 | tf_op jit(solution)/shard_map/psum | solution.py:132
  691.7 0.8 broadcast_multiply_fusion
  (158 shorter events, 7.4 us)
Async XLA Ops:
  7.2 1.1 copy-start
  7.2 82.5 %all-gather.5.cloned.1.call-start = ((), (), s32[]{:S(2)}) async-start(), calls=%async_computation.2 | async-start | bytes 3342336 | tf_op jit(solution)/shard_map/all_gather | solution.py:62
  45.0 5.5 copy-start.8
  45.0 6.6 copy-start.9
  45.1 112.9 %reduce-scatter.2.cloned.1.call-start = ((), (), s32[]{:S(2)}) async-start(), calls=%async_computation.4 | async-start | bytes 3342336 | tf_op jit(solution)/shard_map/reduce_scatter | solution.py:83
  50.5 151.8 %all-gather.7.cloned.1.call-start = ((), (), s32[]{:S(2)}) async-start(), calls=%async_computation.3 | async-start | bytes 1671168 | tf_op jit(solution)/shard_map/all_gather | solution.py:76
  99.5 102.8 %copy-start.7 = (bf16[1,192,512]{2,1,0:T(8,128)(2,1)S(1)}, bf16[1,192,512]{2,1,0:T(8,128)(2,1)}, u32[]{:S(2)}) copy-start(bf16[1,192,512]{2,1,0:T(8,128)(2,1)} %param.16) | copy-start | bytes 589828
  99.6 61.3 %copy-start.3 = (f32[192,256]{1,0:T(8,128)}, f32[192,256]{1,0:T(8,128)S(1)}, u32[]{:S(2)}) copy-start(f32[192,256]{1,0:T(8,128)S(1)} %get-tuple-element.84) | copy-start | bytes 589828
  159.1 48.0 %copy-start.4 = (f32[192,256]{1,0:T(8,128)}, f32[192,256]{1,0:T(8,128)S(1)}, u32[]{:S(2)}) copy-start(f32[192,256]{1,0:T(8,128)S(1)} %get-tuple-element.79) | copy-start | bytes 589828
  161.0 46.1 %copy-start.2 = (f32[192,256]{1,0:T(8,128)}, f32[192,256]{1,0:T(8,128)S(1)}, u32[]{:S(2)}) copy-start(f32[192,256]{1,0:T(8,128)S(1)} %mul.459) | copy-start | bytes 589828
  164.2 150.0 %all-reduce.9.cloned.1.call-start = ((), (), s32[]{:S(2)}) async-start(), calls=%async_computation.5 | async-start | bytes 8388608 | tf_op jit(solution)/shard_map/psum | solution.py:108
  207.1 213.9 %all-gather.9.cloned.1.call-start = ((), (), s32[]{:S(2)}) async-start(), calls=%async_computation.6 | async-start | bytes 4456448 | tf_op jit(solution)/shard_map/all_gather | solution.py:115
  320.6 106.8 %all-to-all-start = ((bf16[16,256,512]{1,2,0:T(8,128)(2,1)}), bf16[16,256,512]{1,2,0:T(8,128)(2,1)}, u32[]{:S(2)}, u32[]{:S(2)}) async-start(bf16[16,256,512]{1,2,0:T(8,128)(2,1)} %copy.22), calls=%async_computation.1 | async-start | bytes 8388608 | tf_op jit(solution)/shard_map/all_to_all | solution.py:112
  326.2 210.8 %all-reduce.11.cloned.1.call-start = ((), (), s32[]{:S(2)}) async-start(), calls=%async_computation.7 | async-start | bytes 524288 | tf_op jit(solution)/shard_map/psum | solution.py:120
  433.2 222.7 %all-gather.11.cloned.1.call-start = ((), (), s32[]{:S(2)}) async-start(), calls=%async_computation.8 | async-start | bytes 2228224 | tf_op jit(solution)/shard_map/all_gather | solution.py:129
  434.0 193.8 %copy-start.1 = (bf16[192,4096]{1,0:T(8,128)(2,1)S(1)}, bf16[192,4096]{1,0:T(8,128)(2,1)}, u32[]{:S(2)}) copy-start(bf16[192,4096]{1,0:T(8,128)(2,1)} %all-gather.7.cloned.1.call-done) | copy-start | bytes 4718596
  539.9 0.7 copy-start.6
  616.6 15.0 %copy-start.5 = (bf16[256,256]{0,1:T(8,128)(2,1)S(1)}, bf16[256,256]{0,1:T(8,128)(2,1)}, u32[]{:S(2)}) copy-start(bf16[256,256]{0,1:T(8,128)(2,1)} %fusion.19) | copy-start | bytes 393220
Sparse Core Ops, SparseCore 0:
  45.2 44.4 all-gather.4
  93.5 64.4 reduce-scatter.1
  164.4 37.9 all-gather.6
  207.2 106.9 all-reduce.8
  316.4 104.4 all-gather.8
  433.3 103.7 all-reduce.10
  614.1 41.7 all-gather.10
where the time goes:
time: 700 us; the launch traced here: 699 us
  waiting for transfers between devices  466 us (67%)
  other arithmetic  73.8 us (11%)
  blocking collectives  71.5 us (10%)
  matrix products  39.3 us (6%)
  local copies, waits for them, and re-layouts  26.9 us (4%)
  between operations  15.8 us (2%)
    psum x1, waiting for transfers between devices, per_device(): lax.psum(grad_part.astype(jnp.bfloat16), 'dp').astype(jnp.float32)  107 us
    psum x1, waiting for transfers between devices, per_device(): gram_matrix = lax.psum(gram_local, 'fsdp')  103 us
    all_gather x1, waiting for transfers between devices, per_device(): lax.all_gather(right_prev, 'fsdp', axis=0, tiled=True)  94.7 us
    reduce_scatter x1, waiting for transfers between devices, per_device(): lax.psum_scatter(jnp.einsum('cd,ld->cl', weight_rows, cot_cols, preferred...  58.3 us
    all_gather x1, waiting for transfers between devices, per_device(): shard_piece = lax.all_gather(gated_out, 'fsdp', axis=1, tiled=True)  38 us
    another operation x7, other arithmetic, per_device(): lower_factor = jnp.linalg.cholesky(gram_matrix)  36.4 us
    psum x1, blocking collectives, per_device(): square_sums = lax.psum(jnp.sum(x_cols * x_cols, axis=1), 'fsdp')  34.9 us
    all_gather x1, waiting for transfers between devices, per_device(): lax.all_gather(normed_cols, 'fsdp', axis=1, tiled=True)  34.7 us
  transfers between devices with their start and end apart: 8, of which 8 were waited for; matrix products, arithmetic and copies ran while one was open for 6% of the time, Pallas kernels for 0%

commit v1 on v0

--- a/solution.py
+++ b/solution.py
@@ -117,7 +117,13 @@
     ).astype(jnp.bfloat16)
     root_scale = jnp.sqrt(jnp.float32(C))
     gram_local = jnp.einsum("cr,cs->rs", panel_own, panel_own, preferred_element_type=jnp.float32)
-    gram_matrix = lax.psum(gram_local, "fsdp")
+    devices = lax.axis_size("fsdp")
+    gram_matrix, reach = (gram_local, 1)
+    while reach < devices:
+        gram_matrix = gram_matrix + lax.ppermute(
+            gram_matrix, "fsdp", [(i, i ^ reach) for i in range(devices)]
+        )
+        reach = 2 * reach
     lower_factor = jnp.linalg.cholesky(gram_matrix)
     solved = jax.scipy.linalg.solve_triangular(
         lower_factor, panel_own.astype(jnp.float32).T, lower=True

time: 700 us -> 643 us (0.919)
  waiting for transfers between devices: 466 us -> 386 us
  starting transfers between devices: 6.13 us -> 27.2 us
    psum x1 -> x0, waiting for transfers between devices: 103 us -> none  [per_device(): gram_matrix = lax.psum(gram_local, 'fsdp')]
    ppermute x0 -> x4, waiting for transfers between devices: none -> 24.6 us  [per_device(): lax.ppermute(gram_matrix, 'fsdp', [(i, i ^ reach) for i in range(devices)])]
    ppermute x0 -> x4, starting transfers between devices: none -> 21.1 us  [per_device(): lax.ppermute(gram_matrix, 'fsdp', [(i, i ^ reach) for i in range(devices)])]
  transfers between devices with their start and end apart: 8 -> 11, of which waited for: 8 -> 11; matrix products, arithmetic and copies ran while one was open for 6% -> 6% of each run, Pallas kernels for 0% -> 0%
where the time goes in v1:
time: 643 us; the launch traced here: 642 us
  waiting for transfers between devices  386 us (60%)
  other arithmetic  75.2 us (12%)
  blocking collectives  71.5 us (11%)
  matrix products  40.3 us (6%)
  starting transfers between devices  27.2 us (4%)
  local copies, waits for them, and re-layouts  25.9 us (4%)
  between operations  15.9 us (2%)
    psum x1, waiting for transfers between devices, per_device(): lax.psum(grad_part.astype(jnp.bfloat16), 'dp').astype(jnp.float32)  107 us
    all_gather x1, waiting for transfers between devices, per_device(): lax.all_gather(right_prev, 'fsdp', axis=0, tiled=True)  94.5 us
    reduce_scatter x1, waiting for transfers between devices, per_device(): lax.psum_scatter(jnp.einsum('cd,ld->cl', weight_rows, cot_cols, preferred...  58.3 us
    all_gather x1, waiting for transfers between devices, per_device(): shard_piece = lax.all_gather(gated_out, 'fsdp', axis=1, tiled=True)  38 us
    another operation x7, other arithmetic, per_device(): lower_factor = jnp.linalg.cholesky(gram_matrix)  37.1 us
    psum x1, blocking collectives, per_device(): square_sums = lax.psum(jnp.sum(x_cols * x_cols, axis=1), 'fsdp')  34.9 us
    all_gather x1, waiting for transfers between devices, per_device(): lax.all_gather(normed_cols, 'fsdp', axis=1, tiled=True)  34.7 us
    psum x1, blocking collectives, per_device(): column_sums = lax.psum(jnp.sum(right_raw * right_raw, axis=0), 'fsdp')  31.6 us
  transfers between devices with their start and end apart: 11, of which 11 were waited for; matrix products, arithmetic and copies ran while one was open for 6% of the time, Pallas kernels for 0%

profile of v1, /device:TPU:0, one launch (start us, length us, event | category | flops | bytes accessed | tf_op | source)
XLA Modules:
  0.0 642.2 jit_solution(10323132610793809353)
XLA Ops:
  7.2 0.7 convert_element_type.108
  8.2 1.1 multiply_reduce_fusion.1
  9.3 34.9 %psum.28 = f32[192]{0:T(256)S(1)} all-reduce(f32[192]{0:T(256)S(1)} %get-tuple-element.121), channel_id=1, replica_groups=mesh['dp'=2,'fsdp'=16] {'fsdp'}, use_global_device_ids=true, to_apply=%region_1.0 | all-reduce | flops 192 | bytes 1536 | tf_op jit(solution)/shard_map/psum | solution.py:55
  44.2 0.8 multiply_convert_fusion
  45.1 5.4 fusion.14
  55.0 34.7 %all-gather.5.cloned.1.call-done = bf16[192,8192]{1,0:T(8,128)(2,1)} async-done(((bf16[192,512]{1,0:T(8,128)(2,1)}), bf16[192,8192]{1,0:T(8,128)(2,1)}) %all-gather.5.cloned.1.call-update) | async-done | bytes 3145744 | tf_op jit(solution)/shard_map/all_gather | solution.py:62
  89.7 9.8 %fusion.6 = bf16[3,192,256]{2,1,0:T(8,128)(2,1)S(1)} fusion(bf16[3,256,8192]{2,1,0:T(8,128)(2,1)} %param.12, bf16[192,8192]{1,0:T(8,128)(2,1)} %all-gather.5.cloned.1.call-done), kind=kOutput, calls=%fused_computation.8 | convolution fusion | flops 2416066560 | bytes 16023552 | tf_op jit(solution)/shard_map/ld,kcd->klc/dot_general | solution.py:60
  99.6 58.3 %reduce-scatter.2.cloned.1.call-done = f32[256,192]{0,1:T(8,128)} async-done(((f32[4096,192]{0,1:T(8,128)}), f32[256,192]{0,1:T(8,128)}) %reduce-scatter.2.cloned.1.call-update) | async-done | bytes 196624 | tf_op jit(solution)/shard_map/reduce_scatter | solution.py:83
  158.0 1.1 bitcast_multiply_fusion
  159.1 1.0 fusion.28
  160.1 0.8 fusion.29
  161.0 2.6 multiply_reduce_fusion.23
  163.6 0.7 multiply_convert_fusion.1
  164.3 38.0 %all-gather.7.cloned.1.call-done = bf16[192,4096]{1,0:T(8,128)(2,1)} async-done(((bf16[192,256]{1,0:T(8,128)(2,1)}), bf16[192,4096]{1,0:T(8,128)(2,1)}) %all-gather.7.cloned.1.call-update) | async-done | bytes 1572880 | tf_op jit(solution)/shard_map/all_gather | solution.py:76
  202.3 4.7 convolution_convert_fusion
  207.7 106.5 %all-reduce.8.cloned.1.call-done = bf16[4096,512]{1,0:T(8,128)(2,1)} async-done(((bf16[4096,512]{1,0:T(8,128)(2,1)}), bf16[4096,512]{1,0:T(8,128)(2,1)}) %all-reduce.8.cloned.1.call-update) | async-done | bytes 4194320 | tf_op jit(solution)/shard_map/psum | solution.py:108
  314.2 6.4 copy.24
  320.6 5.7 all-to-all-start
  326.5 94.5 %all-gather.9.cloned.1.call-done = bf16[8192,256]{1,0:T(8,128)(2,1)} async-done(((bf16[512,256]{1,0:T(8,128)(2,1)}), bf16[8192,256]{1,0:T(8,128)(2,1)}) %all-gather.9.cloned.1.call-update) | async-done | bytes 4194320 | tf_op jit(solution)/shard_map/all_gather | solution.py:115
  421.0 6.5 %all-to-all-done = bf16[16,256,512]{1,2,0:T(8,128)(2,1)} async-done(((bf16[16,256,512]{1,2,0:T(8,128)(2,1)}), bf16[16,256,512]{1,2,0:T(8,128)(2,1)}, u32[]{:S(2)}, u32[]{:S(2)}) %all-to-all-start) | async-done | bytes 4194336 | tf_op jit(solution)/shard_map/all_to_all | solution.py:112
  427.4 4.8 convolution_convert_fusion.1
  432.7 1.3 collective-permute-done
  434.1 6.2 collective-permute-start.1
  440.3 6.7 %collective-permute-done.1 = f32[256,256]{0,1:T(8,128)S(1)} collective-permute-done((f32[256,256]{0,1:T(8,128)S(1)}, f32[256,256]{0,1:T(8,128)S(1)}, u32[]{:S(2)}, u32[]{:S(2)}) %collective-permute-start.1) | collective-permute-done | bytes 262176 | tf_op jit(solution)/shard_map/ppermute | solution.py:123
  447.1 11.8 %collective-permute-start.2 = (f32[256,256]{0,1:T(8,128)S(1)}, f32[256,256]{0,1:T(8,128)S(1)}, u32[]{:S(2)}, u32[]{:S(2)}) collective-permute-start(f32[256,256]{0,1:T(8,128)S(1)} %add.194), channel_id=1, source_target_pairs={{0,4},{1,5},{2,6},{3,7},{4,0},{5,1},{6,2},{7,3},{8,12},{9,13},{10,... | collective-permute-start | bytes 786440 | tf_op jit(solution)/shard_map/ppermute | solution.py:123
  458.8 6.1 collective-permute-done.2
  465.0 2.7 collective-permute-start.3
  468.3 10.5 %collective-permute-done.3 = f32[256,256]{0,1:T(8,128)S(1)} collective-permute-done((f32[256,256]{0,1:T(8,128)S(1)}, f32[256,256]{0,1:T(8,128)S(1)}, u32[]{:S(2)}, u32[]{:S(2)}) %collective-permute-start.3) | collective-permute-done | bytes 262176 | tf_op jit(solution)/shard_map/ppermute | solution.py:123
  478.9 0.8 copy.27
  479.7 1.0 fusion.12
  480.7 0.7 copy-done.8
  481.4 11.7 %cholesky.50 = f32[128,128]{1,0:T(8,128)S(1)} custom-call(f32[128,128]{1,0:T(8,128)S(1)} %cholesky.118), custom_call_target="Cholesky" | custom-call | tf_op jit(solution)/shard_map/jit(cholesky)/cholesky | solution.py:127
  493.1 0.6 select_reduce_fusion.1
  493.7 0.7 cholesky.113
  494.4 10.4 %custom-call.15 = f32[1,128,128]{1,2,0:T(8,128)} custom-call(f32[1,128,128]{2,1,0:T(8,128)S(1)} %get-tuple-element.89), custom_call_target="InvertDiagBlocksLowerTriangular" | custom-call | tf_op jit(solution)/shard_map/jit(cholesky)/cholesky | solution.py:127
  504.9 1.7 constant_dynamic-update-slice_fusion.29
  506.6 1.1 slice_subtract_fusion
  507.7 11.7 %cholesky.105 = f32[128,128]{1,0:T(8,128)S(1)} custom-call(f32[128,128]{1,0:T(8,128)S(1)} %slice_subtract_fusion), custom_call_target="Cholesky" | custom-call | tf_op jit(solution)/shard_map/jit(cholesky)/cholesky | solution.py:127
  519.4 1.3 compare_reduce_fusion.1
  520.7 0.6 select_reduce_fusion
  521.3 0.6 compare_reduce_fusion
  523.2 1.7 select_select_fusion
  524.9 0.7 triangular_solve.59
  525.6 6.8 %while.1 = (s32[]{:T(128)}, f32[256,256]{1,0:T(8,128)}, s32[2,2]{1,0:T(2,128)S(1)}, f32[2,128,128]{2,1,0:T(8,128)}, s32[]{:T(128)}) while((s32[]{:T(128)}, f32[256,256]{1,0:T(8,128)}, s32[2,2]{1,0:T(2,128)S(1)}, f32[2,128,128]{2,1,0:T(8,128)}, s32[]{:T(128)}) %tuple.107), condition=%wide.while_cond, body=%wide.while_body.sunk | while | flops 2 | bytes 132205 | solution.py:128
  525.6 0.6 fusion.49
  526.2 2.9 bitcast_dynamic-update-slice_fusion.2
  529.7 2.8 bitcast_dynamic-update-slice_fusion.2
  532.5 21.1 %custom-call.16 = f32[2,128,128]{1,2,0:T(8,128)} custom-call(f32[2,128,128]{2,1,0:T(8,128)} %get-tuple-element.11), custom_call_target="InvertDiagBlocksLowerTriangular" | custom-call | tf_op jit(solution)/shard_map/jit(_solve_triangular)/triangular_solve | solution.py:128
  553.6 1.1 fusion.22
  554.7 1.2 convolution_subtract_fusion
  555.9 1.2 fusion.21
  557.1 0.7 fusion.19
  557.8 2.0 multiply_reduce_fusion.2
  560.5 2.0 multiply_reduce_fusion.29
  564.0 0.7 stack.112
  564.7 0.8 stack.113
  566.0 5.0 psum.29
  571.0 0.6 copy.29
  571.6 3.8 fusion.9
  575.5 0.8 copy.30
  576.2 22.5 %all-gather.11.cloned.1.call-done = bf16[4096,256]{0,1:T(8,128)(2,1)} async-done(((bf16[256,256]{0,1:T(8,128)(2,1)}), bf16[4096,256]{0,1:T(8,128)(2,1)}) %all-gather.11.cloned.1.call-update) | async-done | bytes 2097168 | tf_op jit(solution)/shard_map/all_gather | solution.py:135
  598.8 4.2 multiply_reduce_fusion
  602.9 31.6 %psum.31 = f32[256]{0:T(256)S(1)} all-reduce(f32[256]{0:T(256)S(1)} %get-tuple-element.125), channel_id=1, replica_groups=mesh['dp'=2,'fsdp'=16] {'fsdp'}, use_global_device_ids=true, to_apply=%region_42.43 | all-reduce | flops 256 | bytes 2048 | tf_op jit(solution)/shard_map/psum | solution.py:138
  634.5 0.8 broadcast_multiply_fusion
  (171 shorter events, 10.2 us)
Async XLA Ops:
  7.2 1.1 copy-start
  7.2 82.5 %all-gather.5.cloned.1.call-start = ((), (), s32[]{:S(2)}) async-start(), calls=%async_computation.2 | async-start | bytes 3342336 | tf_op jit(solution)/shard_map/all_gather | solution.py:62
  45.0 5.5 copy-start.10
  45.0 6.6 %copy-start.11 = (f32[16,7]{0,1:T(8,128)S(1)}, f32[16,7]{0,1:T(8,128)}, u32[]{:S(2)}) copy-start(f32[16,7]{0,1:T(8,128)} %param.14) | copy-start | bytes 1348
  45.1 112.9 %reduce-scatter.2.cloned.1.call-start = ((), (), s32[]{:S(2)}) async-start(), calls=%async_computation.4 | async-start | bytes 3342336 | tf_op jit(solution)/shard_map/reduce_scatter | solution.py:83
  50.5 151.8 %all-gather.7.cloned.1.call-start = ((), (), s32[]{:S(2)}) async-start(), calls=%async_computation.3 | async-start | bytes 1671168 | tf_op jit(solution)/shard_map/all_gather | solution.py:76
  99.5 102.8 %copy-start.9 = (bf16[1,192,512]{2,1,0:T(8,128)(2,1)S(1)}, bf16[1,192,512]{2,1,0:T(8,128)(2,1)}, u32[]{:S(2)}) copy-start(bf16[1,192,512]{2,1,0:T(8,128)(2,1)} %param.16) | copy-start | bytes 589828
  99.6 61.3 %copy-start.5 = (f32[192,256]{1,0:T(8,128)}, f32[192,256]{1,0:T(8,128)S(1)}, u32[]{:S(2)}) copy-start(f32[192,256]{1,0:T(8,128)S(1)} %get-tuple-element.84) | copy-start | bytes 589828
  99.6 107.4 %copy-start.2 = (f32[192,256]{1,0:T(8,128)}, f32[192,256]{1,0:T(8,128)S(1)}, u32[]{:S(2)}) copy-start(f32[192,256]{1,0:T(8,128)S(1)} %get-tuple-element.83) | copy-start | bytes 589828
  159.1 48.0 %copy-start.6 = (f32[192,256]{1,0:T(8,128)}, f32[192,256]{1,0:T(8,128)S(1)}, u32[]{:S(2)}) copy-start(f32[192,256]{1,0:T(8,128)S(1)} %get-tuple-element.79) | copy-start | bytes 589828
  161.0 46.1 %copy-start.4 = (f32[192,256]{1,0:T(8,128)}, f32[192,256]{1,0:T(8,128)S(1)}, u32[]{:S(2)}) copy-start(f32[192,256]{1,0:T(8,128)S(1)} %mul.459) | copy-start | bytes 589828
  164.2 150.0 %all-reduce.8.cloned.1.call-start = ((), (), s32[]{:S(2)}) async-start(), calls=%async_computation.5 | async-start | bytes 8388608 | tf_op jit(solution)/shard_map/psum | solution.py:108
  207.1 213.9 %all-gather.9.cloned.1.call-start = ((), (), s32[]{:S(2)}) async-start(), calls=%async_computation.6 | async-start | bytes 4456448 | tf_op jit(solution)/shard_map/all_gather | solution.py:115
  320.6 106.8 %all-to-all-start = ((bf16[16,256,512]{1,2,0:T(8,128)(2,1)}), bf16[16,256,512]{1,2,0:T(8,128)(2,1)}, u32[]{:S(2)}, u32[]{:S(2)}) async-start(bf16[16,256,512]{1,2,0:T(8,128)(2,1)} %copy.24), calls=%async_computation.1 | async-start | bytes 8388608 | tf_op jit(solution)/shard_map/all_to_all | solution.py:112
  326.3 272.5 %all-gather.11.cloned.1.call-start = ((), (), s32[]{:S(2)}) async-start(), calls=%async_computation.7 | async-start | bytes 2228224 | tf_op jit(solution)/shard_map/all_gather | solution.py:135
  432.4 1.6 collective-permute-start
  434.1 13.0 %collective-permute-start.1 = (f32[256,256]{0,1:T(8,128)S(1)}, f32[256,256]{0,1:T(8,128)S(1)}, u32[]{:S(2)}, u32[]{:S(2)}) collective-permute-start(f32[256,256]{0,1:T(8,128)S(1)} %add.193), channel_id=1, source_target_pairs={{0,2},{1,3},{2,0},{3,1},{4,6},{5,7},{6,4},{7,5},{8,10},{9,11},{10,... | collective-permute-start | bytes 786440 | tf_op jit(solution)/shard_map/ppermute | solution.py:123
  447.1 17.9 %collective-permute-start.2 = (f32[256,256]{0,1:T(8,128)S(1)}, f32[256,256]{0,1:T(8,128)S(1)}, u32[]{:S(2)}, u32[]{:S(2)}) collective-permute-start(f32[256,256]{0,1:T(8,128)S(1)} %add.194), channel_id=1, source_target_pairs={{0,4},{1,5},{2,6},{3,7},{4,0},{5,1},{6,2},{7,3},{8,12},{9,13},{10,... | collective-permute-start | bytes 786440 | tf_op jit(solution)/shard_map/ppermute | solution.py:123
  465.0 13.8 %collective-permute-start.3 = (f32[256,256]{0,1:T(8,128)S(1)}, f32[256,256]{0,1:T(8,128)S(1)}, u32[]{:S(2)}, u32[]{:S(2)}) collective-permute-start(f32[256,256]{0,1:T(8,128)S(1)} %add.195), channel_id=1, source_target_pairs={{0,8},{1,9},{2,10},{3,11},{4,12},{5,13},{6,14},{7,15},{8,0},{9,1},... | collective-permute-start | bytes 786440 | tf_op jit(solution)/shard_map/ppermute | solution.py:123
  478.9 92.8 %copy-start.1 = (bf16[192,4096]{1,0:T(8,128)(2,1)S(1)}, bf16[192,4096]{1,0:T(8,128)(2,1)}, u32[]{:S(2)}) copy-start(bf16[192,4096]{1,0:T(8,128)(2,1)} %all-gather.7.cloned.1.call-done) | copy-start | bytes 4718596
  480.7 0.7 copy-start.8
  481.4 79.0 %copy-start.3 = (f32[192,256]{1,0:T(8,128)S(1)}, f32[192,256]{1,0:T(8,128)}, u32[]{:S(2)}) copy-start(f32[192,256]{1,0:T(8,128)} %copy-done.2) | copy-start | bytes 589828
  560.5 15.0 %copy-start.7 = (bf16[256,256]{0,1:T(8,128)(2,1)S(1)}, bf16[256,256]{0,1:T(8,128)(2,1)}, u32[]{:S(2)}) copy-start(bf16[256,256]{0,1:T(8,128)(2,1)} %fusion.19) | copy-start | bytes 393220
Sparse Core Ops, SparseCore 0:
  45.2 44.4 all-gather.4
  93.5 64.4 reduce-scatter.1
  164.4 37.9 all-gather.6
  207.2 106.9 all-reduce.7
  316.5 104.4 all-gather.8
  557.9 40.8 all-gather.10
